TPU v7x, 512 devices: a whole 4x8x8 slice. The times are simulated.
512 devices in a mesh: tok: 64 (over z, y_hi, x), feat: 8 (over y_lo, core).
Axes of the slice: x: 4, y: 8 (y_hi: 2, y_lo: 4; y = y_hi * 4 + y_lo), z: 8, core: 2. Of those that a mesh axis runs over, the one named last changes fastest.
Arguments:
- activations: bfloat16 [131072, 8192], P('tok', 'feat')
- labels: int32 [131072], P('tok'), may hold values from 0 to 7, as said below
Outputs:
- cov_panel: float32 [1024, 8192], P('tok', 'feat')
- cross_cov: float32 [8, 8192], P(None, 'feat')
Inputs may be any that keep to these rules, and one draw needn't show every extreme that they name: `labels`: each token's class.
All inputs are finite; a program needn't handle non-finite values.
Results may differ from a plain program's by a relative error of at most 0.0017.
Values may be sent and summed in bfloat16 or wider, within the bound.
A program may use at most 64 MiB of HBM per device.

v0:
```python
import jax
import jax.numpy as jnp
from jax import lax
from jax.sharding import PartitionSpec as P

CLASSES = 8
PANEL = 128


def tokens_product(left, right):
    return lax.dot_general(
        left, right, (((0,), (0,)), ((), ())), preferred_element_type=jnp.float32
    )


def body(activations, labels):
    tok_rows = activations.shape[0]
    total = tok_rows * lax.axis_size("tok")
    column_total = lax.psum(jnp.sum(activations, axis=0, dtype=jnp.float32), "tok")
    mean = column_total / total
    centered = (activations.astype(jnp.float32) - mean).astype(jnp.bfloat16)
    onehot = (labels[:, None] == jnp.arange(CLASSES, dtype=jnp.int32)[None, :]).astype(jnp.bfloat16)
    class_part = tokens_product(onehot, centered)
    class_total = lax.psum(class_part, "tok")
    cross_cov = class_total / total
    outgoing = centered[:, :PANEL]
    panel = lax.all_gather(outgoing, "feat", axis=1, tiled=True)
    summed = lax.psum_scatter(
        tokens_product(panel, centered), "tok", scatter_dimension=0, tiled=True
    )
    cov_panel = summed / (total - 1)
    return (cov_panel, cross_cov)


def solution(mesh):
    in_specs = (P("tok", "feat"), P("tok"))
    out_specs = (P("tok", "feat"), P(None, "feat"))
    return jax.shard_map(body, mesh=mesh, in_specs=in_specs, out_specs=out_specs, check_vma=False)
```

profile of v0, /device:TPU:8, one launch (start us, length us, event | category | flops | bytes accessed | tf_op | source)
XLA Modules:
  0.0 762.9 jit_solution(16792029753697239541)
XLA Ops:
  7.2 0.0 all-gather.2.cloned.1.call-start
  7.2 2.9 convert_reduce_fusion
  10.1 230.5 %psum.14 = f32[1024]{0:T(1024)S(1)} all-reduce(f32[1024]{0:T(1024)S(1)} %convert_reduce_fusion), channel_id=1, replica_groups=mesh['tok'=64,'feat'=8] {'tok'}, use_global_device_ids=true, to_apply=%region_1.0 | all-reduce | flops 1024 | bytes 8192 | tf_op jit(solution)/shard_map/psum | solution.py:19
  240.5 3.3 fusion
  243.9 0.0 copy-start
  243.9 1.9 copy-done
  245.8 0.9 slice.4
  246.7 0.0 all-gather.2.cloned.1.call-update
  246.8 0.0 reduce-scatter.2.cloned.1.call-start
  246.8 45.1 %all-gather.2.cloned.1.call-done = bf16[2048,1024]{1,0:T(8,128)(2,1)} async-done(((bf16[2048,128]{1,0:T(8,128)(2,1)}), bf16[2048,1024]{1,0:T(8,128)(2,1)}) %all-gather.2.cloned.1.call-update) | async-done | bytes 4194320 | tf_op jit(solution)/shard_map/all_gather | solution.py:27
  291.9 10.0 %fusion.3 = f32[1024,1024]{1,0:T(8,128)} fusion(bf16[2048,1024]{1,0:T(8,128)(2,1)} %all-gather.2.cloned.1.call-done, bf16[2048,1024]{1,0:T(8,128)(2,1)} %copy-done), kind=kOutput, calls=%fused_computation.9 | convolution fusion | flops 4294967296 | bytes 12582912 | tf_op jit(solution)/shard_map/dot_general | solution.py:11
  301.9 0.0 copy-start.1
  301.9 0.0 reduce-scatter.2.cloned.1.call-update
  301.9 0.7 copy-done.1
  302.6 3.1 fusion.1
  305.7 437.9 %psum.15 = f32[8,1024]{1,0:T(8,128)S(1)} all-reduce(f32[8,1024]{1,0:T(8,128)S(1)} %fusion.1), channel_id=1, replica_groups=mesh['tok'=64,'feat'=8] {'tok'}, use_global_device_ids=true, to_apply=%region_3.0 | all-reduce | flops 8192 | bytes 65536 | tf_op jit(solution)/shard_map/psum | solution.py:24
  743.7 0.6 broadcast_multiply_fusion.1
  744.3 10.3 %reduce-scatter.2.cloned.1.call-done = f32[16,1024]{1,0:T(8,128)} async-done(((f32[1024,1024]{1,0:T(8,128)}), f32[16,1024]{1,0:T(8,128)}) %reduce-scatter.2.cloned.1.call-update) | async-done | bytes 65552 | tf_op jit(solution)/shard_map/reduce_scatter | solution.py:28
  754.6 1.5 broadcast_multiply_fusion
  (1 shorter events, 0.0 us)
Async XLA Ops:
  7.2 284.7 %all-gather.2.cloned.1.call-start = ((), (), s32[]{:S(2)}) async-start(), calls=%async_computation.1 | async-start | bytes 4718592 | tf_op jit(solution)/shard_map/all_gather | solution.py:27
  243.9 1.9 copy-start
  246.8 507.8 %reduce-scatter.2.cloned.1.call-start = ((), (), s32[]{:S(2)}) async-start(), calls=%async_computation.2 | async-start | bytes 4259840 | tf_op jit(solution)/shard_map/reduce_scatter | solution.py:28
  301.9 0.7 copy-start.1
Sparse Core Ops, SparseCore 0:
  246.9 44.9 all-gather.1
  302.0 452.4 reduce-scatter.1
where the time goes:
time: 763 us
  blocking collectives  668 us (88%)
  waiting for transfers between devices  55.4 us (7%)
  between operations  14.1 us (2%)
  matrix products  13.1 us (2%)
  other arithmetic  8.3 us (1%)
    psum x1, blocking collectives, body(): class_total = lax.psum(class_part, 'tok')  438 us
    psum x1, blocking collectives, body(): lax.psum(jnp.sum(activations, axis=0, dtype=jnp.float32), 'tok')  230 us
    all_gather x1, waiting for transfers between devices, body(): panel = lax.all_gather(outgoing, 'feat', axis=1, tiled=True)  45.1 us
  transfers between devices with their start and end apart: 2, of which 2 were waited for; matrix products, arithmetic and copies ran while one was open for 0% of the time, Pallas kernels for 0%

commit v1 on v0

--- a/solution.py
+++ b/solution.py
@@ -21,7 +21,7 @@
     centered = (activations.astype(jnp.float32) - mean).astype(jnp.bfloat16)
     onehot = (labels[:, None] == jnp.arange(CLASSES, dtype=jnp.int32)[None, :]).astype(jnp.bfloat16)
     class_part = tokens_product(onehot, centered)
-    class_total = lax.psum(class_part, "tok")
+    class_total = jnp.sum(lax.all_gather(class_part, "tok"), axis=0)
     cross_cov = class_total / total
     outgoing = centered[:, :PANEL]
     panel = lax.all_gather(outgoing, "feat", axis=1, tiled=True)

time: 763 us -> 890 us (1.17)
  waiting for transfers between devices: 55.4 us -> 618 us
  blocking collectives: 668 us -> 230 us
    psum x1 -> x0, blocking collectives: 438 us -> none  [body(): class_total = lax.psum(class_part, 'tok')]
    reduce_scatter x1, waiting for transfers between devices: 10.3 us -> 446 us  [body(): lax.psum_scatter(tokens_product(panel, centered), 'tok', scatter_dimensio...]
    all_gather x0 -> x1, waiting for transfers between devices: none -> 131 us  [body(): class_total = jnp.sum(lax.all_gather(class_part, 'tok'), axis=0)]
  transfers between devices with their start and end apart: 2 -> 3, of which waited for: 2 -> 3; matrix products, arithmetic and copies ran while one was open for 0% -> 2% of each run, Pallas kernels for 0% -> 0%
where the time goes in v1:
time: 890 us; the launch traced here: 889 us
  waiting for transfers between devices  618 us (69%)
  blocking collectives  230 us (26%)
  matrix products  13.8 us (2%)
  between operations  13.8 us (2%)
  other arithmetic  10 us (1%)
    reduce_scatter x1, waiting for transfers between devices, body(): lax.psum_scatter(tokens_product(panel, centered), 'tok', scatter_dimensio...  446 us
    psum x1, blocking collectives, body(): lax.psum(jnp.sum(activations, axis=0, dtype=jnp.float32), 'tok')  230 us
    all_gather x1, waiting for transfers between devices, body(): class_total = jnp.sum(lax.all_gather(class_part, 'tok'), axis=0)  131 us
    all_gather x1, waiting for transfers between devices, body(): panel = lax.all_gather(outgoing, 'feat', axis=1, tiled=True)  41.2 us
  transfers between devices with their start and end apart: 3, of which 3 were waited for; matrix products, arithmetic and copies ran while one was open for 2% of the time, Pallas kernels for 0%

profile of v1, /device:TPU:8, one launch (start us, length us, event | category | flops | bytes accessed | tf_op | source)
XLA Modules:
  0.0 889.5 jit_solution(3463979111080537623)
XLA Ops:
  7.2 0.0 all-gather.4.cloned.1.call-start
  7.2 2.9 convert_reduce_fusion
  10.1 230.5 %psum.7 = f32[1024]{0:T(1024)S(1)} all-reduce(f32[1024]{0:T(1024)S(1)} %convert_reduce_fusion), channel_id=1, replica_groups=mesh['tok'=64,'feat'=8] {'tok'}, use_global_device_ids=true, to_apply=%region_1.0 | all-reduce | flops 1024 | bytes 8192 | tf_op jit(solution)/shard_map/psum | solution.py:19
  240.5 0.0 copy-start.1
  240.5 3.3 fusion
  243.9 0.0 copy-start
  243.9 1.9 copy-done
  245.8 1.0 slice.4
  246.8 0.0 all-gather.4.cloned.1.call-update
  246.8 0.0 all-gather.6.cloned.1.call-start
  246.9 0.0 copy-done.1
  246.9 3.8 fusion.1
  250.7 0.0 all-gather.6.cloned.1.call-update
  250.7 0.0 reduce-scatter.2.cloned.1.call-start
  250.7 41.2 %all-gather.4.cloned.1.call-done = bf16[2048,1024]{1,0:T(8,128)(2,1)} async-done(((bf16[2048,128]{1,0:T(8,128)(2,1)}), bf16[2048,1024]{1,0:T(8,128)(2,1)}) %all-gather.4.cloned.1.call-update) | async-done | bytes 4194320 | tf_op jit(solution)/shard_map/all_gather | solution.py:27
  292.0 10.0 %fusion.3 = f32[1024,1024]{1,0:T(8,128)} fusion(bf16[2048,1024]{1,0:T(8,128)(2,1)} %all-gather.4.cloned.1.call-done, bf16[2048,1024]{1,0:T(8,128)(2,1)} %copy-done), kind=kOutput, calls=%fused_computation.10 | convolution fusion | flops 4294967296 | bytes 12582912 | tf_op jit(solution)/shard_map/dot_general | solution.py:11
  302.0 0.0 reduce-scatter.2.cloned.1.call-update
  302.0 131.4 %all-gather.6.cloned.1.call-done = f32[512,1024]{1,0:T(8,128)} async-done(((f32[8,1024]{1,0:T(8,128)}), f32[512,1024]{1,0:T(8,128)}) %all-gather.6.cloned.1.call-update) | async-done | bytes 2097168 | tf_op jit(solution)/shard_map/all_gather | solution.py:24
  433.4 1.7 bitcast_reduce_fusion
  435.1 0.6 broadcast_multiply_fusion.1
  435.7 445.8 %reduce-scatter.2.cloned.1.call-done = f32[16,1024]{1,0:T(8,128)} async-done(((f32[1024,1024]{1,0:T(8,128)}), f32[16,1024]{1,0:T(8,128)}) %reduce-scatter.2.cloned.1.call-update) | async-done | bytes 65552 | tf_op jit(solution)/shard_map/reduce_scatter | solution.py:28
  881.5 1.5 broadcast_multiply_fusion
  (1 shorter events, 0.0 us)
Async XLA Ops:
  7.2 284.8 %all-gather.4.cloned.1.call-start = ((), (), s32[]{:S(2)}) async-start(), calls=%async_computation.1 | async-start | bytes 4718592 | tf_op jit(solution)/shard_map/all_gather | solution.py:27
  240.5 6.3 copy-start.1
  243.9 1.9 copy-start
  246.8 186.5 %all-gather.6.cloned.1.call-start = ((), (), s32[]{:S(2)}) async-start(), calls=%async_computation.3 | async-start | bytes 2129920 | tf_op jit(solution)/shard_map/all_gather | solution.py:24
  250.7 630.8 %reduce-scatter.2.cloned.1.call-start = ((), (), s32[]{:S(2)}) async-start(), calls=%async_computation.2 | async-start | bytes 4259840 | tf_op jit(solution)/shard_map/reduce_scatter | solution.py:28
Sparse Core Ops, SparseCore 0:
  246.9 44.9 all-gather.3
  297.0 136.3 all-gather.5
  436.2 445.2 reduce-scatter.1

commit v2 on v0

--- a/solution.py
+++ b/solution.py
@@ -24,7 +24,9 @@
     class_total = lax.psum(class_part, "tok")
     cross_cov = class_total / total
     outgoing = centered[:, :PANEL]
-    panel = lax.all_gather(outgoing, "feat", axis=1, tiled=True)
+    panel = jnp.concatenate(
+        lax.all_to_all(jnp.stack([outgoing] * lax.axis_size("feat")), "feat", 0, 0), axis=1
+    )
     summed = lax.psum_scatter(
         tokens_product(panel, centered), "tok", scatter_dimension=0, tiled=True
     )

time: 763 us -> 800 us (1.048)
  blocking collectives: 668 us -> 755 us
  waiting for transfers between devices: 55.4 us -> 8.65 us
    all_to_all x0 -> x1, blocking collectives: none -> 95.6 us  [body(): lax.all_to_all(jnp.stack([outgoing] * lax.axis_size('feat')), 'feat', 0, 0)]
    all_gather x1 -> x0, waiting for transfers between devices: 45.1 us -> none  [body(): panel = lax.all_gather(outgoing, 'feat', axis=1, tiled=True)]
    psum x1, blocking collectives: 438 us -> 429 us  [body(): class_total = lax.psum(class_part, 'tok')]
  transfers between devices with their start and end apart: 2 -> 1, of which waited for: 2 -> 1; matrix products, arithmetic and copies ran while one was open for 0% -> 0% of each run, Pallas kernels for 0% -> 0%
where the time goes in v2:
time: 800 us; the launch traced here: 799 us
  blocking collectives  755 us (94%)
  between operations  14.1 us (2%)
  matrix products  9.18 us (1%)
  waiting for transfers between devices  8.65 us (1%)
  other arithmetic  8.3 us (1%)
    psum x1, blocking collectives, body(): class_total = lax.psum(class_part, 'tok')  429 us
    psum x1, blocking collectives, body(): lax.psum(jnp.sum(activations, axis=0, dtype=jnp.float32), 'tok')  231 us
    all_to_all x1, blocking collectives, body(): lax.all_to_all(jnp.stack([outgoing] * lax.axis_size('feat')), 'feat', 0, 0)  95.6 us
  transfers between devices with their start and end apart: 1, of which 1 were waited for; matrix products, arithmetic and copies ran while one was open for 0% of the time, Pallas kernels for 0%

profile of v2, /device:TPU:8, one launch (start us, length us, event | category | flops | bytes accessed | tf_op | source)
XLA Modules:
  0.0 799.2 jit_solution(10261682642671693419)
XLA Ops:
  7.2 0.0 reduce-scatter.2.cloned.1.call-start
  7.2 2.9 convert_reduce_fusion
  10.1 230.6 %psum.14 = f32[1024]{0:T(1024)S(1)} all-reduce(f32[1024]{0:T(1024)S(1)} %convert_reduce_fusion), channel_id=1, replica_groups=mesh['tok'=64,'feat'=8] {'tok'}, use_global_device_ids=true, to_apply=%region_1.0 | all-reduce | flops 1024 | bytes 8192 | tf_op jit(solution)/shard_map/psum | solution.py:19
  240.6 3.3 fusion
  244.0 0.0 copy-start
  244.0 1.9 copy-done
  245.9 0.1 slice.4
  246.1 0.2 copy.4
  246.3 0.5 stack.2
  246.8 0.0 copy-start.1
  246.8 95.6 %all_to_all.5 = bf16[8,2048,128]{1,2,0:T(8,128)(2,1)S(1)} all-to-all(bf16[8,2048,128]{1,2,0:T(8,128)(2,1)S(1)} %stack.2), channel_id=1, replica_groups=mesh['tok'=64,'feat'=8] {'feat'}, dimensions={0} | all-to-all | bytes 8388608 | tf_op jit(solution)/shard_map/all_to_all | solution.py:28
  342.4 0.0 copy-done.1
  342.4 6.0 fusion.3
  348.5 0.0 copy-start.2
  348.5 0.0 reduce-scatter.2.cloned.1.call-update
  348.5 0.7 copy-done.2
  349.2 3.1 fusion.1
  352.3 429.3 %psum.15 = f32[8,1024]{1,0:T(8,128)S(1)} all-reduce(f32[8,1024]{1,0:T(8,128)S(1)} %fusion.1), channel_id=1, replica_groups=mesh['tok'=64,'feat'=8] {'tok'}, use_global_device_ids=true, to_apply=%region_3.0 | all-reduce | flops 8192 | bytes 65536 | tf_op jit(solution)/shard_map/psum | solution.py:24
  781.6 0.6 broadcast_multiply_fusion.1
  782.2 8.6 %reduce-scatter.2.cloned.1.call-done = f32[16,1024]{1,0:T(8,128)} async-done(((f32[1024,1024]{1,0:T(8,128)}), f32[16,1024]{1,0:T(8,128)}) %reduce-scatter.2.cloned.1.call-update) | async-done | bytes 65552 | tf_op jit(solution)/shard_map/reduce_scatter | solution.py:30
  790.9 1.5 broadcast_multiply_fusion
  (1 shorter events, 0.0 us)
Async XLA Ops:
  7.2 783.7 %reduce-scatter.2.cloned.1.call-start = ((), (), s32[]{:S(2)}) async-start(), calls=%async_computation.2 | async-start | bytes 4259840 | tf_op jit(solution)/shard_map/reduce_scatter | solution.py:30
  244.0 1.9 copy-start
  246.8 95.6 %copy-start.1 = (bf16[2048,1024]{1,0:T(8,128)(2,1)S(1)}, bf16[2048,1024]{1,0:T(8,128)(2,1)}, u32[]{:S(2)}) copy-start(bf16[2048,1024]{1,0:T(8,128)(2,1)} %copy-done) | copy-start | bytes 12582916
  348.5 0.7 copy-start.2
Sparse Core Ops, SparseCore 0:
  348.6 442.2 reduce-scatter.1
